TPU v7x, 32 devices: a whole 2x2x4 slice. The times are simulated.
32 devices in a mesh: row: 4 (over y, x), col: 8 (over z, core).
Axes of the slice: x: 2, y: 2, z: 4, core: 2. Of those that a mesh axis runs over, the one named last changes fastest.
Arguments:
- momentum: float32 [4608, 8192], P('row', 'col'), may hold values from -37 to 37
Outputs:
- update: float32 [4608, 8192], P('row', 'col')
All inputs are finite; a program needn't handle non-finite values.
Results may differ from a plain program's by a relative error of at most 0.0049.
Values may be sent and summed in bfloat16 or wider, within the bound.
No kernel may reach another device: no remote copies, remote signals or barrier semaphores. Data moves between devices by JAX's collectives and lax.ppermute only.
A program may use at most 128 MiB of HBM per device.

v0:
```python
import math
import jax
import jax.numpy as jnp
from jax import lax
from jax.sharding import PartitionSpec as P

ROWS = 4608
COLS = 8192
quintic_a = 3.4445
quintic_b = -4.775
quintic_c = 2.0315


def from_root(shard, axis, root):
    mine = lax.axis_index(axis) == root
    return lax.psum(jnp.where(mine, shard, jnp.zeros_like(shard)), axis)


def rows_product(left, right):
    return lax.dot_general(
        left, right, (((1,), (1,)), ((), ())), preferred_element_type=jnp.float32
    )


def body(momentum):
    partial_sum = jnp.sum(momentum * momentum)
    norm_squares = lax.psum(partial_sum, ("row", "col"))
    factor = 0.6 * math.sqrt(ROWS) / (jnp.sqrt(norm_squares) + 1e-07)
    scaled = (momentum * factor).astype(jnp.bfloat16)
    tile_ratio = lax.axis_size("col") // lax.axis_size("row")
    col_index = lax.axis_index("col")
    source_row = col_index // tile_ratio
    half_index = col_index % tile_ratio
    row_panel = lax.all_gather(scaled, "col", axis=1, tiled=True)
    part_rows = row_panel.shape[0] // tile_ratio
    own_part = lax.dynamic_slice_in_dim(row_panel, half_index * part_rows, part_rows, 0)
    peer_rows = from_root(own_part, "row", source_row)
    gram = rows_product(row_panel, peer_rows).astype(jnp.bfloat16)
    gram_panel = lax.all_gather(gram, "col", axis=1, tiled=True)
    gram_columns = lax.all_gather(gram, "row", axis=0, tiled=True)
    squared = jnp.dot(gram_panel, gram_columns, preferred_element_type=jnp.float32)
    poly = (quintic_b * gram.astype(jnp.float32) + quintic_c * squared).astype(jnp.bfloat16)
    poly_panel = lax.all_gather(poly, "col", axis=1, tiled=True)
    product = jnp.dot(
        poly_panel,
        lax.all_gather(scaled, "row", axis=0, tiled=True),
        preferred_element_type=jnp.float32,
    )
    return math.sqrt(COLS) * (quintic_a * scaled.astype(jnp.float32) + product)


def solution(mesh):
    placed = (P("row", "col"),)
    return jax.shard_map(
        body, mesh=mesh, in_specs=placed, out_specs=P("row", "col"), check_vma=False
    )
```

profile of v0, /device:TPU:0, one launch (start us, length us, event | category | flops | bytes accessed | tf_op | source)
XLA Modules:
  0.0 828.4 jit_solution(4937114119938713192)
XLA Ops:
  6.5 0.0 all-gather.6.cloned.1.call-start
  6.5 4.2 multiply_reduce_fusion
  10.7 42.2 %psum.14 = f32[]{:T(128)} all-reduce(f32[]{:T(128)} %multiply_reduce_fusion), channel_id=1, replica_groups=mesh['row'=4,'col'=8] {'row','col'}, use_global_device_ids=true, to_apply=%region_1.0 | all-reduce | flops 1 | bytes 8 | tf_op jit(solution)/shard_map/psum | solution.py:27
  53.6 4.4 multiply_convert_fusion
  58.0 0.0 all-gather.6.cloned.1.call-update
  58.0 0.0 all-reduce.2.cloned.1.call-start
  58.1 168.3 %all-gather.6.cloned.1.call-done = bf16[1152,8192]{1,0:T(8,128)(2,1)} async-done(((bf16[1152,1024]{1,0:T(8,128)(2,1)}), bf16[1152,8192]{1,0:T(8,128)(2,1)}) %all-gather.6.cloned.1.call-update) | async-done | bytes 18874384 | tf_op jit(solution)/shard_map/all_gather | solution.py:34
  226.5 9.8 %dynamic-slice_select_fusion = bf16[576,8192]{1,0:T(8,128)(2,1)} fusion(bf16[1152,8192]{1,0:T(8,128)(2,1)} %all-gather.6.cloned.1.call-done, s32[]{:T(128)S(6)} %select_n.25, pred[]{:T(512)S(6)} %eq.5), kind=kLoop, calls=%fused_computation | loop fusion | flops 4718592 | bytes 18874372 | tf_op jit(solution)/shard_map/jit(_where)/select_n | solution.py:16
  236.2 0.0 all-reduce.2.cloned.1.call-update
  236.2 0.0 all-gather.10.cloned.1.call-start
  236.3 186.7 %all-reduce.2.cloned.1.call-done = bf16[576,8192]{1,0:T(8,128)(2,1)} async-done(((bf16[576,8192]{1,0:T(8,128)(2,1)}), bf16[576,8192]{1,0:T(8,128)(2,1)}) %all-reduce.2.cloned.1.call-update) | async-done | bytes 9437200 | tf_op jit(solution)/shard_map/psum | solution.py:16
  423.0 18.8 %convolution_convert_fusion = bf16[1152,576]{0,1:T(8,128)(2,1)} fusion(bf16[1152,8192]{1,0:T(8,128)(2,1)} %all-gather.6.cloned.1.call-done, bf16[576,8192]{1,0:T(8,128)(2,1)} %all-reduce.2.cloned.1.call-done), kind=kOutput, calls=%fused_computation.7 | convolution fusion | flops 10872299520 | bytes 29638656 | tf_op jit(solution)/shard_map/dot_general | solution.py:20
  441.8 0.0 all-gather.10.cloned.1.call-update
  441.9 0.0 all-gather.8.cloned.1.call-start
  441.9 0.5 all-gather.8.cloned.1.call-update
  442.4 0.0 all-gather.14.cloned.1.call-start
  442.5 0.5 all-gather.14.cloned.1.call-update
  443.0 0.0 copy-start
  443.0 0.2 all-gather.12.cloned.1.call-start
  443.3 60.6 %all-gather.10.cloned.1.call-done = bf16[4608,576]{0,1:T(8,128)(2,1)} async-done(((bf16[1152,576]{0,1:T(8,128)(2,1)}), bf16[4608,576]{0,1:T(8,128)(2,1)}) %all-gather.10.cloned.1.call-update) | async-done | bytes 5308432 | tf_op jit(solution)/shard_map/all_gather | solution.py:40
  503.9 102.0 %all-gather.8.cloned.1.call-done = bf16[1152,4608]{0,1:T(8,128)(2,1)} async-done(((bf16[1152,576]{0,1:T(8,128)(2,1)}), bf16[1152,4608]{0,1:T(8,128)(2,1)}) %all-gather.8.cloned.1.call-update) | async-done | bytes 10616848 | tf_op jit(solution)/shard_map/all_gather | solution.py:39
  605.9 13.1 %fusion.2 = bf16[1152,576]{0,1:T(8,128)(2,1)} fusion(bf16[4608,576]{0,1:T(8,128)(2,1)} %all-gather.10.cloned.1.call-done, bf16[1152,4608]{0,1:T(8,128)(2,1)} %all-gather.8.cloned.1.call-done, bf16[1152,576]{0,1:T(8,128)(2,1)} %convolution_convert_fusion), kind=kOutput, calls=%fused_computation.8 | convolution fusion | flops 6118612992 | bytes 18579456 | tf_op jit(solution)/shard_map/dot_general | solution.py:41
  618.9 0.0 all-gather.12.cloned.1.call-update
  619.0 83.1 %all-gather.14.cloned.1.call-done = bf16[4608,1024]{1,0:T(8,128)(2,1)} async-done(((bf16[1152,1024]{1,0:T(8,128)(2,1)}), bf16[4608,1024]{1,0:T(8,128)(2,1)}) %all-gather.14.cloned.1.call-update) | async-done | bytes 9437200 | tf_op jit(solution)/shard_map/all_gather | solution.py:46
  702.1 102.0 %all-gather.12.cloned.1.call-done = bf16[1152,4608]{0,1:T(8,128)(2,1)} async-done(((bf16[1152,576]{0,1:T(8,128)(2,1)}), bf16[1152,4608]{0,1:T(8,128)(2,1)}) %all-gather.12.cloned.1.call-update) | async-done | bytes 10616848 | tf_op jit(solution)/shard_map/all_gather | solution.py:43
  804.1 0.0 copy-done
  804.1 17.5 %fusion = f32[1152,1024]{1,0:T(8,128)} fusion(bf16[1152,4608]{0,1:T(8,128)(2,1)} %all-gather.12.cloned.1.call-done, bf16[4608,1024]{1,0:T(8,128)(2,1)} %all-gather.14.cloned.1.call-done, bf16[1152,1024]{1,0:T(8,128)(2,1)S(1)} %copy-done), kind=kOutput, calls=%fused_computation.2 | convolution fusion | flops 10876354560 | bytes 27131904 | tf_op jit(solution)/shard_map/dot_general | solution.py:44
Async XLA Ops:
  6.5 219.9 %all-gather.6.cloned.1.call-start = ((), (), s32[]{:S(2)}) async-start(), calls=%async_computation | async-start | bytes 21233664 | tf_op jit(solution)/shard_map/all_gather | solution.py:34
  58.0 365.0 %all-reduce.2.cloned.1.call-start = ((), (), s32[]{:S(2)}) async-start(), calls=%async_computation.1 | async-start | bytes 18874368 | tf_op jit(solution)/shard_map/psum | solution.py:16
  236.2 267.6 %all-gather.10.cloned.1.call-start = ((), (), s32[]{:S(2)}) async-start(), calls=%async_computation.3 | async-start | bytes 6635520 | tf_op jit(solution)/shard_map/all_gather | solution.py:40
  441.9 164.0 %all-gather.8.cloned.1.call-start = ((), (), s32[]{:S(2)}) async-start(), calls=%async_computation.2 | async-start | bytes 11943936 | tf_op jit(solution)/shard_map/all_gather | solution.py:39
  442.4 259.7 %all-gather.14.cloned.1.call-start = ((), (), s32[]{:S(2)}) async-start(), calls=%async_computation.5 | async-start | bytes 11796480 | tf_op jit(solution)/shard_map/all_gather | solution.py:46
  443.0 361.1 %copy-start = (bf16[1152,1024]{1,0:T(8,128)(2,1)S(1)}, bf16[1152,1024]{1,0:T(8,128)(2,1)}, u32[]{:S(2)}) copy-start(bf16[1152,1024]{1,0:T(8,128)(2,1)} %multiply_convert_fusion) | copy-start | bytes 7077892
  443.0 361.0 %all-gather.12.cloned.1.call-start = ((), (), s32[]{:S(2)}) async-start(), calls=%async_computation.4 | async-start | bytes 11943936 | tf_op jit(solution)/shard_map/all_gather | solution.py:43
Sparse Core Ops, SparseCore 0:
  58.2 168.2 all-gather.5
  236.4 186.5 all-reduce.1
  442.0 61.8 all-gather.9
  505.4 100.4 all-gather.7
  607.5 94.5 all-gather.13
  703.6 100.4 all-gather.11
where the time goes:
time: 829 us; the launch traced here: 828 us
  waiting for transfers between devices  704 us (85%)
  matrix products  49.4 us (6%)
  blocking collectives  42.2 us (5%)
  other arithmetic  18.3 us (2%)
  between operations  14.2 us (2%)
    psum x1, waiting for transfers between devices, from_root(): return lax.psum(jnp.where(mine, shard, jnp.zeros_like(shard)), axis)  187 us
    all_gather x1, waiting for transfers between devices, body(): row_panel = lax.all_gather(scaled, 'col', axis=1, tiled=True)  168 us
    all_gather x1, waiting for transfers between devices, body(): gram_panel = lax.all_gather(gram, 'col', axis=1, tiled=True)  102 us
    all_gather x1, waiting for transfers between devices, body(): poly_panel = lax.all_gather(poly, 'col', axis=1, tiled=True)  102 us
    all_gather x1, waiting for transfers between devices, body(): lax.all_gather(scaled, 'row', axis=0, tiled=True)  83.1 us
    all_gather x1, waiting for transfers between devices, body(): gram_columns = lax.all_gather(gram, 'row', axis=0, tiled=True)  60.6 us
    psum x1, blocking collectives, body(): norm_squares = lax.psum(partial_sum, ('row', 'col'))  42.2 us
    dot_general x1, matrix products, rows_product(): lax.dot_general(left, right, (((1,), (1,)), ((), ())), preferred_element_...  18.8 us
  transfers between devices with their start and end apart: 6, of which 6 were waited for; matrix products, arithmetic and copies ran while one was open for 2% of the time, Pallas kernels for 0%

commit v1 on v0

--- a/solution.py
+++ b/solution.py
@@ -37,7 +37,12 @@
     peer_rows = from_root(own_part, "row", source_row)
     gram = rows_product(row_panel, peer_rows).astype(jnp.bfloat16)
     gram_panel = lax.all_gather(gram, "col", axis=1, tiled=True)
-    gram_columns = lax.all_gather(gram, "row", axis=0, tiled=True)
+    ring = [gram]
+    for hop in range(3):
+        ring.append(lax.ppermute(ring[-1], "row", [(dev, (dev + 1) % 4) for dev in range(4)]))
+    gram_columns = jnp.roll(
+        jnp.concatenate(ring[::-1], axis=0), (lax.axis_index("row") + 1) * ring[0].shape[0], axis=0
+    )
     squared = jnp.dot(gram_panel, gram_columns, preferred_element_type=jnp.float32)
     poly = (quintic_b * gram.astype(jnp.float32) + quintic_c * squared).astype(jnp.bfloat16)
     poly_panel = lax.all_gather(poly, "col", axis=1, tiled=True)

time: 829 us -> 765 us (0.923)
  waiting for transfers between devices: 704 us -> 622 us
  local copies, waits for them, and re-layouts: 0.01 us -> 15.2 us
    all_gather x1, waiting for transfers between devices: 102 us -> 0.01 us  [body(): gram_panel = lax.all_gather(gram, 'col', axis=1, tiled=True)]
    ppermute x0 -> x3, waiting for transfers between devices: none -> 91.1 us  [body(): lax.ppermute(ring[-1], 'row', [(dev, (dev + 1) % 4) for dev in range(4)])]
    all_gather x1 -> x0, waiting for transfers between devices: 60.6 us -> none  [body(): gram_columns = lax.all_gather(gram, 'row', axis=0, tiled=True)]
    unnamed x2 -> x11, local copies, waits for them, and re-layouts: 0.01 us -> 13.9 us
    all_gather x1, waiting for transfers between devices: 83.1 us -> 73.1 us  [body(): lax.all_gather(scaled, 'row', axis=0, tiled=True)]
  transfers between devices with their start and end apart: 6 -> 8, of which waited for: 6 -> 7; matrix products, arithmetic and copies ran while one was open for 2% -> 4% of each run, Pallas kernels for 0% -> 0%
where the time goes in v1:
time: 765 us
  waiting for transfers between devices  622 us (81%)
  matrix products  51 us (7%)
  blocking collectives  42.2 us (6%)
  other arithmetic  18.3 us (2%)
  local copies, waits for them, and re-layouts  15.2 us (2%)
  between operations  13.9 us (2%)
    psum x1, waiting for transfers between devices, from_root(): return lax.psum(jnp.where(mine, shard, jnp.zeros_like(shard)), axis)  187 us
    all_gather x1, waiting for transfers between devices, body(): row_panel = lax.all_gather(scaled, 'col', axis=1, tiled=True)  168 us
    all_gather x1, waiting for transfers between devices, body(): poly_panel = lax.all_gather(poly, 'col', axis=1, tiled=True)  102 us
    ppermute x3, waiting for transfers between devices, body(): lax.ppermute(ring[-1], 'row', [(dev, (dev + 1) % 4) for dev in range(4)])  91.1 us
    all_gather x1, waiting for transfers between devices, body(): lax.all_gather(scaled, 'row', axis=0, tiled=True)  73.1 us
    psum x1, blocking collectives, body(): norm_squares = lax.psum(partial_sum, ('row', 'col'))  42.2 us
    dot_general x1, matrix products, rows_product(): lax.dot_general(left, right, (((1,), (1,)), ((), ())), preferred_element_...  18.8 us
    dot_general x1, matrix products, body(): jnp.dot(poly_panel, lax.all_gather(scaled, 'row', axis=0, tiled=True), pr...  17.5 us
  transfers between devices with their start and end apart: 8, of which 7 were waited for; matrix products, arithmetic and copies ran while one was open for 4% of the time, Pallas kernels for 0%

profile of v1, /device:TPU:0, one launch (start us, length us, event | category | flops | bytes accessed | tf_op | source)
XLA Modules:
  0.0 764.7 jit_solution(13011157864566619945)
XLA Ops:
  6.5 0.0 all-gather.5.cloned.1.call-start
  6.5 4.2 multiply_reduce_fusion
  10.7 42.2 %psum.14 = f32[]{:T(128)} all-reduce(f32[]{:T(128)} %multiply_reduce_fusion), channel_id=1, replica_groups=mesh['row'=4,'col'=8] {'row','col'}, use_global_device_ids=true, to_apply=%region_1.0 | all-reduce | flops 1 | bytes 8 | tf_op jit(solution)/shard_map/psum | solution.py:27
  53.6 4.4 multiply_convert_fusion
  58.0 0.0 all-gather.5.cloned.1.call-update
  58.0 0.0 all-reduce.2.cloned.1.call-start
  58.1 168.3 %all-gather.5.cloned.1.call-done = bf16[1152,8192]{1,0:T(8,128)(2,1)} async-done(((bf16[1152,1024]{1,0:T(8,128)(2,1)}), bf16[1152,8192]{1,0:T(8,128)(2,1)}) %all-gather.5.cloned.1.call-update) | async-done | bytes 18874384 | tf_op jit(solution)/shard_map/all_gather | solution.py:34
  226.4 9.8 %dynamic-slice_select_fusion = bf16[576,8192]{1,0:T(8,128)(2,1)} fusion(bf16[1152,8192]{1,0:T(8,128)(2,1)} %all-gather.5.cloned.1.call-done, s32[]{:T(128)S(6)} %select_n.37, pred[]{:T(512)S(6)} %eq.8), kind=kLoop, calls=%fused_computation | loop fusion | flops 4718592 | bytes 18874372 | tf_op jit(solution)/shard_map/jit(_where)/select_n | solution.py:16
  236.2 0.0 all-reduce.2.cloned.1.call-update
  236.2 0.0 all-gather.7.cloned.1.call-start
  236.3 186.7 %all-reduce.2.cloned.1.call-done = bf16[576,8192]{1,0:T(8,128)(2,1)} async-done(((bf16[576,8192]{1,0:T(8,128)(2,1)}), bf16[576,8192]{1,0:T(8,128)(2,1)}) %all-reduce.2.cloned.1.call-update) | async-done | bytes 9437200 | tf_op jit(solution)/shard_map/psum | solution.py:16
  423.0 18.8 %convolution_convert_fusion = bf16[1152,576]{0,1:T(8,128)(2,1)} fusion(bf16[1152,8192]{1,0:T(8,128)(2,1)} %all-gather.5.cloned.1.call-done, bf16[576,8192]{1,0:T(8,128)(2,1)} %all-reduce.2.cloned.1.call-done), kind=kOutput, calls=%fused_computation.10 | convolution fusion | flops 10872299520 | bytes 29638656 | tf_op jit(solution)/shard_map/dot_general | solution.py:20
  441.8 0.0 copy-start.1
  441.8 0.0 all-gather.7.cloned.1.call-update
  441.8 0.0 all-gather.11.cloned.1.call-start
  441.8 0.5 all-gather.11.cloned.1.call-update
  442.4 0.0 all-gather.9.cloned.1.call-start
  442.4 1.5 collective-permute-start
  443.9 30.4 %collective-permute-done = bf16[1152,576]{0,1:T(8,128)(2,1)S(1)} collective-permute-done((bf16[1152,576]{0,1:T(8,128)(2,1)}, bf16[1152,576]{0,1:T(8,128)(2,1)S(1)}, u32[]{:S(2)}, u32[]{:S(2)}) %collective-permute-start) | collective-permute-done | bytes 1327136 | tf_op jit(solution)/shard_map/ppermute | solution.py:42
  474.3 0.6 collective-permute-start.1
  474.9 30.4 %collective-permute-done.1 = bf16[1152,576]{0,1:T(8,128)(2,1)} collective-permute-done((bf16[1152,576]{0,1:T(8,128)(2,1)S(1)}, bf16[1152,576]{0,1:T(8,128)(2,1)}, u32[]{:S(2)}, u32[]{:S(2)}) %collective-permute-start.1) | collective-permute-done | bytes 1327136 | tf_op jit(solution)/shard_map/ppermute | solution.py:42
  505.3 0.0 collective-permute-start.2
  505.3 30.3 %collective-permute-done.2 = bf16[1152,576]{0,1:T(8,128)(2,1)} collective-permute-done((bf16[1152,576]{0,1:T(8,128)(2,1)}, bf16[1152,576]{0,1:T(8,128)(2,1)}, u32[]{:S(2)}, u32[]{:S(2)}) %collective-permute-start.2) | collective-permute-done | bytes 1327136 | tf_op jit(solution)/shard_map/ppermute | solution.py:42
  535.6 2.6 constant_dynamic-update-slice_fusion.7
  538.2 2.5 constant_dynamic-update-slice_fusion.6
  540.7 1.3 constant_dynamic-update-slice_fusion.5
  542.0 0.0 copy-done.1
  542.0 1.2 constant_dynamic-update-slice_fusion.4
  543.3 2.5 constant_dynamic-update-slice_fusion.3
  545.8 2.5 constant_dynamic-update-slice_fusion.2
  548.3 1.2 constant_dynamic-update-slice_fusion.1
  549.5 1.2 constant_dynamic-update-slice_fusion
  550.8 0.0 copy-start
  550.8 0.0 all-gather.7.cloned.1.call-done
  550.8 14.7 %fusion.9 = bf16[1152,576]{0,1:T(8,128)(2,1)} fusion(bf16[1152,4608]{0,1:T(8,128)(2,1)} %all-gather.7.cloned.1.call-done, bf16[9216,576]{0,1:T(8,128)(2,1)} %constant_dynamic-update-slice_fusion, s32[]{:T(128)S(6)} %select_n.40, bf16[1152,576]{0,1:T(8,128)(2,1)} %convolution_convert_fusion), kind=kOutput, calls=%fused_computation.9 | convolution fusion | flops 6118612992 | bytes 18579460 | tf_op jit(solution)/shard_map/dot_general | solution.py:46
  565.5 0.0 all-gather.9.cloned.1.call-update
  565.5 73.1 %all-gather.11.cloned.1.call-done = bf16[4608,1024]{1,0:T(8,128)(2,1)} async-done(((bf16[1152,1024]{1,0:T(8,128)(2,1)}), bf16[4608,1024]{1,0:T(8,128)(2,1)}) %all-gather.11.cloned.1.call-update) | async-done | bytes 9437200 | tf_op jit(solution)/shard_map/all_gather | solution.py:51
  638.7 102.0 %all-gather.9.cloned.1.call-done = bf16[1152,4608]{0,1:T(8,128)(2,1)} async-done(((bf16[1152,576]{0,1:T(8,128)(2,1)}), bf16[1152,4608]{0,1:T(8,128)(2,1)}) %all-gather.9.cloned.1.call-update) | async-done | bytes 10616848 | tf_op jit(solution)/shard_map/all_gather | solution.py:48
  740.7 0.0 copy-done
  740.7 17.5 %fusion.2 = f32[1152,1024]{1,0:T(8,128)} fusion(bf16[1152,4608]{0,1:T(8,128)(2,1)} %all-gather.9.cloned.1.call-done, bf16[4608,1024]{1,0:T(8,128)(2,1)} %all-gather.11.cloned.1.call-done, bf16[1152,1024]{1,0:T(8,128)(2,1)S(1)} %copy-done), kind=kOutput, calls=%fused_computation.4 | convolution fusion | flops 10876354560 | bytes 27131904 | tf_op jit(solution)/shard_map/dot_general | solution.py:49
Async XLA Ops:
  6.5 219.9 %all-gather.5.cloned.1.call-start = ((), (), s32[]{:S(2)}) async-start(), calls=%async_computation | async-start | bytes 21233664 | tf_op jit(solution)/shard_map/all_gather | solution.py:34
  58.0 365.0 %all-reduce.2.cloned.1.call-start = ((), (), s32[]{:S(2)}) async-start(), calls=%async_computation.1 | async-start | bytes 18874368 | tf_op jit(solution)/shard_map/psum | solution.py:16
  236.2 314.5 %all-gather.7.cloned.1.call-start = ((), (), s32[]{:S(2)}) async-start(), calls=%async_computation.2 | async-start | bytes 11943936 | tf_op jit(solution)/shard_map/all_gather | solution.py:39
  441.8 100.3 %copy-start.1 = (bf16[1152,576]{0,1:T(8,128)(2,1)S(1)}, bf16[1152,576]{0,1:T(8,128)(2,1)}, u32[]{:S(2)}) copy-start(bf16[1152,576]{0,1:T(8,128)(2,1)} %convolution_convert_fusion) | copy-start | bytes 3981316
  441.8 196.9 %all-gather.11.cloned.1.call-start = ((), (), s32[]{:S(2)}) async-start(), calls=%async_computation.4 | async-start | bytes 11796480 | tf_op jit(solution)/shard_map/all_gather | solution.py:51
  442.4 298.3 %all-gather.9.cloned.1.call-start = ((), (), s32[]{:S(2)}) async-start(), calls=%async_computation.3 | async-start | bytes 11943936 | tf_op jit(solution)/shard_map/all_gather | solution.py:48
  442.4 31.9 %collective-permute-start = (bf16[1152,576]{0,1:T(8,128)(2,1)}, bf16[1152,576]{0,1:T(8,128)(2,1)S(1)}, u32[]{:S(2)}, u32[]{:S(2)}) collective-permute-start(bf16[1152,576]{0,1:T(8,128)(2,1)} %convolution_convert_fusion), channel_id=1, source_target_pairs={{0,8},{8,16},{16,24},{24,0},{1,9},{9,17},{17,25},{25,1},{2,10},{10... | collective-permute-start | bytes 3981320 | tf_op jit(solution)/shard_map/ppermute | solution.py:42
  474.3 31.0 %collective-permute-start.1 = (bf16[1152,576]{0,1:T(8,128)(2,1)S(1)}, bf16[1152,576]{0,1:T(8,128)(2,1)}, u32[]{:S(2)}, u32[]{:S(2)}) collective-permute-start(bf16[1152,576]{0,1:T(8,128)(2,1)S(1)} %collective-permute-done), channel_id=1, source_target_pairs={{0,8},{8,16},{16,24},{24,0},{1,9},{9,17},{17,25},{25,1},{2,10},{10... | collective-permute-start | bytes 3981320 | tf_op jit(solution)/shard_map/ppermute | solution.py:42
  505.3 30.3 %collective-permute-start.2 = (bf16[1152,576]{0,1:T(8,128)(2,1)}, bf16[1152,576]{0,1:T(8,128)(2,1)}, u32[]{:S(2)}, u32[]{:S(2)}) collective-permute-start(bf16[1152,576]{0,1:T(8,128)(2,1)} %collective-permute-done.1), channel_id=1, source_target_pairs={{0,8},{8,16},{16,24},{24,0},{1,9},{9,17},{17,25},{25,1},{2,10},{10... | collective-permute-start | bytes 3981320 | tf_op jit(solution)/shard_map/ppermute | solution.py:42
  550.8 189.9 %copy-start = (bf16[1152,1024]{1,0:T(8,128)(2,1)S(1)}, bf16[1152,1024]{1,0:T(8,128)(2,1)}, u32[]{:S(2)}) copy-start(bf16[1152,1024]{1,0:T(8,128)(2,1)} %multiply_convert_fusion) | copy-start | bytes 7077892
Sparse Core Ops, SparseCore 0:
  58.1 168.2 all-gather.4
  236.3 186.5 all-reduce.1
  441.9 100.4 all-gather.6
  544.1 94.5 all-gather.10
  640.2 100.4 all-gather.8
